TPU v7x, 32 devices: a whole 2x2x4 slice. The times are simulated.
32 devices in a mesh: member: 2 (over y), tile: 4 (over z), day: 4 (over x, core).
Axes of the slice: x: 2, y: 2, z: 4, core: 2. Of those that a mesh axis runs over, the one named last changes fastest.
Arguments:
- fields: bfloat16 [64, 35, 16384], P(('member', 'day'), None, 'tile'), parts along dimension 0, may hold values from -6 to 6
- remap_tiles: bfloat16 [512, 128, 128], P('tile'), may hold values from 0 to 0.015625
- tile_source: int32 [512], P('tile'), may hold values from 0 to 31, as said below
- tile_band: int32 [512, 1], P('tile'), may hold values from 0 to 3, as said below
- tile_block: int32 [512], P('tile'), may hold values from 0 to 35, as said below
- patterns: bfloat16 [18432, 512], P('tile'), may hold values from -0.125 to 0.125
Outputs:
- scores: float32 [64, 35, 512], P(('member', 'day'), None, 'tile'), parts along dimension 0
There are 2 independent parts, one for each index of `member`. A program takes and returns all parts, laid end to end along the dimension named above; an argument that names none is the same for every part. Nothing has to cross between parts.
Inputs may be any that keep to these rules, and one draw needn't show every extreme that they name: `tile_source`: index of the source block, among the 32 blocks held by the tile's own device; each of those blocks is read by some tile of that device. `tile_band`: among the 128 tiles of one device, at most 64 go to one band, and in some device exactly 64 do. `tile_block`: every target block of every band is written by at least one tile.
All inputs are finite; a program needn't handle non-finite values.
Results may differ from a plain program's by a relative error of at most 0.0039.
Values may be sent and summed in bfloat16 or wider, within the bound.
No kernel may reach another device: no remote copies, remote signals or barrier semaphores. Data moves between devices by JAX's collectives and lax.ppermute only.
A program may use at most 128 MiB of HBM per device.

v0:
```python
import jax
import jax.numpy as jnp
from jax import lax
from jax.sharding import PartitionSpec as P


def on_device(fields, remap_tiles, tile_source, tile_band, tile_block, patterns):
    band_count = lax.axis_size("tile")
    day_count, var_count, source_cells = fields.shape
    tile_count, block_size, _ = remap_tiles.shape
    row_count = day_count * var_count
    source_blocks = source_cells // block_size
    target_blocks = patterns.shape[0] // block_size
    pattern_count = patterns.shape[1]
    pattern_share = pattern_count // band_count
    capacity = max(2, 2 * tile_count // band_count)
    slot_count = band_count * capacity
    blocked = fields.reshape(row_count, source_blocks, block_size)
    columns = jnp.take(blocked, tile_source, axis=1)
    owner = tile_band[:, 0]
    tile_order = jnp.arange(tile_count, dtype=jnp.int32)
    same_owner = owner[:, None] == owner[None, :]
    earlier = tile_order[:, None] > tile_order[None, :]
    rank_within = jnp.sum(jnp.logical_and(same_owner, earlier).astype(jnp.int32), axis=1)
    slot_index = owner * capacity + rank_within
    block_label = (
        jnp.full((slot_count,), -1.0, jnp.bfloat16)
        .at[slot_index]
        .set(tile_block.astype(jnp.bfloat16))
    )
    contrib = jnp.einsum(
        "rtk,tkj->trj", columns, remap_tiles, preferred_element_type=jnp.float32
    ).astype(jnp.bfloat16)
    send_values = (
        jnp.zeros((slot_count, row_count, block_size), jnp.bfloat16).at[slot_index].set(contrib)
    )
    received, label_recv = (
        lax.all_to_all(send_values, "tile", split_axis=0, concat_axis=0, tiled=True),
        lax.all_to_all(block_label, "tile", split_axis=0, concat_axis=0, tiled=True),
    )
    block_ids = jnp.arange(target_blocks, dtype=jnp.int32).astype(jnp.bfloat16)
    selector = (label_recv[None, :] == block_ids[:, None]).astype(jnp.bfloat16)
    remapped = jnp.einsum("bs,srk->rbk", selector, received, preferred_element_type=jnp.float32)
    remapped = remapped.astype(jnp.bfloat16).reshape(row_count, target_blocks * block_size)
    partial_scores = jnp.dot(remapped, patterns, preferred_element_type=jnp.float32)
    total_scores = lax.psum(partial_scores, "tile")
    own_scores = lax.dynamic_slice_in_dim(
        total_scores, lax.axis_index("tile") * pattern_share, pattern_share, 1
    )
    return own_scores.reshape(day_count, var_count, pattern_share)


def solution(mesh):
    return jax.shard_map(
        on_device,
        mesh=mesh,
        in_specs=(
            P(("member", "day"), None, "tile"),
            P("tile", None, None),
            P("tile"),
            P("tile", None),
            P("tile"),
            P("tile", None),
        ),
        out_specs=P(("member", "day"), None, "tile"),
        check_vma=False,
    )
```

profile of v0, /device:TPU:0, one launch (start us, length us, event | category | flops | bytes accessed | tf_op | source)
XLA Modules:
  0.0 542.6 jit_solution(3007958193052604485)
XLA Ops:
  6.5 0.9 convert_reduce_fusion
  7.4 0.7 fusion.21
  8.1 0.7 convert_element_type.25
  8.8 1.3 scatter_custom_fusion.1
  10.1 0.7 all_to_all.12
  10.8 6.3 %all-to-all-start.1 = ((bf16[4,64,1]{1,2,0:T(2,128)(2,1)}), bf16[4,64,1]{1,2,0:T(2,128)(2,1)S(1)}, u32[]{:S(2)}, u32[]{:S(2)}) async-start(bf16[4,64,1]{1,2,0:T(2,128)(2,1)} %all_to_all.12), calls=%async_computation.1 | async-start | bytes 4096 | tf_op jit(solution)/shard_map/all_to_all | solution.py:39
  17.1 0.7 compare_select_fusion
  17.8 0.7 compare_and_fusion
  18.4 2.9 copy.16
  21.4 2.6 reshape.24
  24.0 2.5 copy.17
  26.5 7.1 %gather_fusion = bf16[128,280,128]{2,1,0:T(8,128)(2,1)} fusion(bf16[280,32,128]{2,0,1:T(8,128)(2,1)S(1)} %copy.17, s32[1024]{0:T(1024)S(1)} %pad_clamp_fusion), kind=kCustom, calls=%fused_computation | custom fusion | bytes 18350592 | tf_op jit(solution)/shard_map/jit(_take)/gather | solution.py:19
  33.6 13.4 %fusion.6 = bf16[128,280,128]{2,1,0:T(8,128)(2,1)} fusion(bf16[128,128,128]{2,1,0:T(8,128)(2,1)} %param.7, bf16[128,280,128]{2,1,0:T(8,128)(2,1)} %gather_fusion, pred[128]{0:T(512)(128)(4,1)S(1)} %compare_and_fusion), kind=kOutput, calls=%fused_computation.9 | convolution fusion | flops 1183580160 | bytes 22544512 | tf_op jit(solution)/shard_map/rtk,tkj->trj/dot_general | solution.py:31
  47.0 6.6 %broadcast_in_dim.24 = bf16[256,280,128]{2,1,0:T(8,128)(2,1)} broadcast(bf16[]{:T(256)} %constant.12.clone.1), dimensions={} | broadcast | bytes 18350082 | tf_op jit(solution)/shard_map/broadcast_in_dim | solution.py:35
  53.5 24.0 %scatter_fusion = bf16[256,280,128]{2,1,0:T(8,128)(2,1)} fusion(bf16[256,280,128]{2,1,0:T(8,128)(2,1)} %broadcast_in_dim.24, s32[128]{0:T(128)S(1)} %fusion.21, bf16[128,280,128]{2,1,0:T(8,128)(2,1)} %fusion.6), kind=kCustom, calls=%fused_computation.1 | custom fusion | bytes 27525632 | tf_op jit(solution)/shard_map/scatter | solution.py:35
  77.5 0.0 all-to-all-done.1
  77.5 7.3 %all-to-all-start = ((bf16[256,280,128]{2,1,0:T(8,128)(2,1)}), bf16[256,280,128]{2,1,0:T(8,128)(2,1)}, u32[]{:S(2)}, u32[]{:S(2)}) async-start(bf16[256,280,128]{2,1,0:T(8,128)(2,1)} %scatter_fusion), calls=%async_computation | async-start | bytes 36700160 | tf_op jit(solution)/shard_map/all_to_all | solution.py:38
  84.8 0.2 all-reduce.2.cloned.1.call-start
  85.1 0.1 eq.34
  85.2 396.5 %all-to-all-done = bf16[256,280,128]{2,1,0:T(8,128)(2,1)} async-done(((bf16[256,280,128]{2,1,0:T(8,128)(2,1)}), bf16[256,280,128]{2,1,0:T(8,128)(2,1)}, u32[]{:S(2)}, u32[]{:S(2)}) %all-to-all-start) | async-done | bytes 18350112 | tf_op jit(solution)/shard_map/all_to_all | solution.py:38
  481.7 9.4 %fusion.13 = bf16[280,128,36]{1,2,0:T(8,128)(2,1)S(1)} fusion(bf16[256,280,128]{2,1,0:T(8,128)(2,1)} %all-to-all-done, bf16[256]{0:T(256)(128)(2,1)S(1)} %eq.34, bf16[36]{0:T(256)(128)(2,1)S(1)} %iota_convert_fusion), kind=kOutput, calls=%fused_computation.14 | convolution fusion | flops 661902336 | bytes 20931144 | tf_op jit(solution)/shard_map/bs,srk->rbk/dot_general | solution.py:43
  491.2 4.7 fusion.10
  495.8 0.0 all-reduce.2.cloned.1.call-update
  495.9 38.3 %all-reduce.2.cloned.1.call-done = f32[280,512]{1,0:T(8,128)} async-done(((f32[280,512]{1,0:T(8,128)}), f32[280,512]{1,0:T(8,128)}) %all-reduce.2.cloned.1.call-update) | async-done | bytes 573456 | tf_op jit(solution)/shard_map/psum | solution.py:46
  534.1 0.9 constant_dynamic-slice_fusion
  535.1 0.7 copy.20
  (4 shorter events, 0.0 us)
Async XLA Ops:
  10.8 66.7 %all-to-all-start.1 = ((bf16[4,64,1]{1,2,0:T(2,128)(2,1)}), bf16[4,64,1]{1,2,0:T(2,128)(2,1)S(1)}, u32[]{:S(2)}, u32[]{:S(2)}) async-start(bf16[4,64,1]{1,2,0:T(2,128)(2,1)} %all_to_all.12), calls=%async_computation.1 | async-start | bytes 4096 | tf_op jit(solution)/shard_map/all_to_all | solution.py:39
  77.5 404.2 %all-to-all-start = ((bf16[256,280,128]{2,1,0:T(8,128)(2,1)}), bf16[256,280,128]{2,1,0:T(8,128)(2,1)}, u32[]{:S(2)}, u32[]{:S(2)}) async-start(bf16[256,280,128]{2,1,0:T(8,128)(2,1)} %scatter_fusion), calls=%async_computation | async-start | bytes 36700160 | tf_op jit(solution)/shard_map/all_to_all | solution.py:38
  84.8 449.3 %all-reduce.2.cloned.1.call-start = ((), (), s32[]{:S(2)}) async-start(), calls=%async_computation.2 | async-start | bytes 1146880 | tf_op jit(solution)/shard_map/psum | solution.py:46
Sparse Core Ops, SparseCore 0:
  496.0 38.1 all-reduce.1
where the time goes:
time: 543 us
  waiting for transfers between devices  435 us (80%)
  local copies, waits for them, and re-layouts  49.4 us (9%)
  matrix products  27.5 us (5%)
  starting transfers between devices  13.8 us (3%)
  between operations  13.5 us (2%)
    all_to_all x1, waiting for transfers between devices, on_device(): lax.all_to_all(send_values, 'tile', split_axis=0, concat_axis=0, tiled=True)  397 us
    psum x1, waiting for transfers between devices, on_device(): total_scores = lax.psum(partial_scores, 'tile')  38.3 us
    scatter x1, local copies, waits for them, and re-layouts, on_device(): jnp.zeros((slot_count, row_count, block_size), jnp.bfloat16).at[slot_index]  24 us
    dot_general x1, matrix products, on_device(): jnp.einsum('rtk,tkj->trj', columns, remap_tiles, preferred_element_type=j...  13.4 us
  transfers between devices with their start and end apart: 3, of which 2 were waited for; matrix products, arithmetic and copies ran while one was open for 11% of the time, Pallas kernels for 0%

commit v1 on v0

--- a/solution.py
+++ b/solution.py
@@ -43,7 +43,7 @@
     remapped = jnp.einsum("bs,srk->rbk", selector, received, preferred_element_type=jnp.float32)
     remapped = remapped.astype(jnp.bfloat16).reshape(row_count, target_blocks * block_size)
     partial_scores = jnp.dot(remapped, patterns, preferred_element_type=jnp.float32)
-    total_scores = lax.psum(partial_scores, "tile")
+    total_scores = jnp.sum(lax.all_gather(partial_scores, "tile"), axis=0)
     own_scores = lax.dynamic_slice_in_dim(
         total_scores, lax.axis_index("tile") * pattern_share, pattern_share, 1
     )

time: 543 us -> 555 us (1.022)
  waiting for transfers between devices: 435 us -> 445 us
    all_gather x0 -> x1, waiting for transfers between devices: none -> 48.7 us  [on_device(): total_scores = jnp.sum(lax.all_gather(partial_scores, 'tile'), axis=0)]
    psum x1 -> x0, waiting for transfers between devices: 38.3 us -> none  [on_device(): total_scores = lax.psum(partial_scores, 'tile')]
where the time goes in v1:
time: 555 us; the launch traced here: 554 us
  waiting for transfers between devices  445 us (80%)
  local copies, waits for them, and re-layouts  48.5 us (9%)
  matrix products  27.5 us (5%)
  starting transfers between devices  13.8 us (2%)
  between operations  13.5 us (2%)
    all_to_all x1, waiting for transfers between devices, on_device(): lax.all_to_all(send_values, 'tile', split_axis=0, concat_axis=0, tiled=True)  397 us
    all_gather x1, waiting for transfers between devices, on_device(): total_scores = jnp.sum(lax.all_gather(partial_scores, 'tile'), axis=0)  48.7 us
    scatter x1, local copies, waits for them, and re-layouts, on_device(): jnp.zeros((slot_count, row_count, block_size), jnp.bfloat16).at[slot_index]  24 us
    dot_general x1, matrix products, on_device(): jnp.einsum('rtk,tkj->trj', columns, remap_tiles, preferred_element_type=j...  13.4 us
  transfers between devices with their start and end apart: 3, of which 2 were waited for; matrix products, arithmetic and copies ran while one was open for 11% of the time, Pallas kernels for 0%

profile of v1, /device:TPU:0, one launch (start us, length us, event | category | flops | bytes accessed | tf_op | source)
XLA Modules:
  0.0 554.1 jit_solution(9063448993860377035)
XLA Ops:
  6.5 0.9 convert_reduce_fusion
  7.4 0.7 fusion.21
  8.1 0.7 convert_element_type.25
  8.8 1.3 scatter_custom_fusion.1
  10.1 0.7 all_to_all.12
  10.8 6.3 %all-to-all-start.1 = ((bf16[4,64,1]{1,2,0:T(2,128)(2,1)}), bf16[4,64,1]{1,2,0:T(2,128)(2,1)S(1)}, u32[]{:S(2)}, u32[]{:S(2)}) async-start(bf16[4,64,1]{1,2,0:T(2,128)(2,1)} %all_to_all.12), calls=%async_computation.1 | async-start | bytes 4096 | tf_op jit(solution)/shard_map/all_to_all | solution.py:39
  17.1 0.7 compare_select_fusion
  17.8 0.7 compare_and_fusion
  18.4 2.9 copy.16
  21.4 2.6 reshape.24
  24.0 2.5 copy.17
  26.5 7.1 %gather_fusion = bf16[128,280,128]{2,1,0:T(8,128)(2,1)} fusion(bf16[280,32,128]{2,0,1:T(8,128)(2,1)S(1)} %copy.17, s32[1024]{0:T(1024)S(1)} %pad_clamp_fusion), kind=kCustom, calls=%fused_computation | custom fusion | bytes 18350592 | tf_op jit(solution)/shard_map/jit(_take)/gather | solution.py:19
  33.6 13.4 %fusion.6 = bf16[128,280,128]{2,1,0:T(8,128)(2,1)} fusion(bf16[128,128,128]{2,1,0:T(8,128)(2,1)} %param.7, bf16[128,280,128]{2,1,0:T(8,128)(2,1)} %gather_fusion, pred[128]{0:T(512)(128)(4,1)S(1)} %compare_and_fusion), kind=kOutput, calls=%fused_computation.9 | convolution fusion | flops 1183580160 | bytes 22544512 | tf_op jit(solution)/shard_map/rtk,tkj->trj/dot_general | solution.py:31
  47.0 6.6 %broadcast_in_dim.24 = bf16[256,280,128]{2,1,0:T(8,128)(2,1)} broadcast(bf16[]{:T(256)} %constant.13.clone.1), dimensions={} | broadcast | bytes 18350082 | tf_op jit(solution)/shard_map/broadcast_in_dim | solution.py:35
  53.5 24.0 %scatter_fusion = bf16[256,280,128]{2,1,0:T(8,128)(2,1)} fusion(bf16[256,280,128]{2,1,0:T(8,128)(2,1)} %broadcast_in_dim.24, s32[128]{0:T(128)S(1)} %fusion.21, bf16[128,280,128]{2,1,0:T(8,128)(2,1)} %fusion.6), kind=kCustom, calls=%fused_computation.1 | custom fusion | bytes 27525632 | tf_op jit(solution)/shard_map/scatter | solution.py:35
  77.5 0.0 all-to-all-done.1
  77.5 7.3 %all-to-all-start = ((bf16[256,280,128]{2,1,0:T(8,128)(2,1)}), bf16[256,280,128]{2,1,0:T(8,128)(2,1)}, u32[]{:S(2)}, u32[]{:S(2)}) async-start(bf16[256,280,128]{2,1,0:T(8,128)(2,1)} %scatter_fusion), calls=%async_computation | async-start | bytes 36700160 | tf_op jit(solution)/shard_map/all_to_all | solution.py:38
  84.8 0.2 all-gather.3.cloned.1.call-start
  85.1 0.1 eq.34
  85.2 396.5 %all-to-all-done = bf16[256,280,128]{2,1,0:T(8,128)(2,1)} async-done(((bf16[256,280,128]{2,1,0:T(8,128)(2,1)}), bf16[256,280,128]{2,1,0:T(8,128)(2,1)}, u32[]{:S(2)}, u32[]{:S(2)}) %all-to-all-start) | async-done | bytes 18350112 | tf_op jit(solution)/shard_map/all_to_all | solution.py:38
  481.7 9.4 %fusion.13 = bf16[280,128,36]{1,2,0:T(8,128)(2,1)S(1)} fusion(bf16[256,280,128]{2,1,0:T(8,128)(2,1)} %all-to-all-done, bf16[256]{0:T(256)(128)(2,1)S(1)} %eq.34, bf16[36]{0:T(256)(128)(2,1)S(1)} %iota_convert_fusion), kind=kOutput, calls=%fused_computation.14 | convolution fusion | flops 661902336 | bytes 20931144 | tf_op jit(solution)/shard_map/bs,srk->rbk/dot_general | solution.py:43
  491.2 4.7 fusion.10
  495.8 0.0 all-gather.3.cloned.1.call-update
  495.9 48.7 %all-gather.3.cloned.1.call-done = f32[1120,512]{1,0:T(8,128)} async-done(((f32[280,512]{1,0:T(8,128)}), f32[1120,512]{1,0:T(8,128)}) %all-gather.3.cloned.1.call-update) | async-done | bytes 2293776 | tf_op jit(solution)/shard_map/all_gather | solution.py:46
  544.6 1.9 reduce_sum.22
  546.6 0.7 copy.20
  (5 shorter events, 0.1 us)
Async XLA Ops:
  10.8 66.7 %all-to-all-start.1 = ((bf16[4,64,1]{1,2,0:T(2,128)(2,1)}), bf16[4,64,1]{1,2,0:T(2,128)(2,1)S(1)}, u32[]{:S(2)}, u32[]{:S(2)}) async-start(bf16[4,64,1]{1,2,0:T(2,128)(2,1)} %all_to_all.12), calls=%async_computation.1 | async-start | bytes 4096 | tf_op jit(solution)/shard_map/all_to_all | solution.py:39
  77.5 404.2 %all-to-all-start = ((bf16[256,280,128]{2,1,0:T(8,128)(2,1)}), bf16[256,280,128]{2,1,0:T(8,128)(2,1)}, u32[]{:S(2)}, u32[]{:S(2)}) async-start(bf16[256,280,128]{2,1,0:T(8,128)(2,1)} %scatter_fusion), calls=%async_computation | async-start | bytes 36700160 | tf_op jit(solution)/shard_map/all_to_all | solution.py:38
  84.8 459.7 %all-gather.3.cloned.1.call-start = ((), (), s32[]{:S(2)}) async-start(), calls=%async_computation.2 | async-start | bytes 2867200 | tf_op jit(solution)/shard_map/all_gather | solution.py:46
Sparse Core Ops, SparseCore 0:
  496.0 48.5 all-gather.2
